TPU v7x, 128 devices: a whole 4x4x4 slice. The times are simulated.
128 devices in a mesh: lat: 16 (over z, x_lo, core), vec: 8 (over x_hi, y).
Axes of the slice: x: 4 (x_hi: 2, x_lo: 2; x = x_hi * 2 + x_lo), y: 4, z: 4, core: 2. Of those that a mesh axis runs over, the one named last changes fastest.
Arguments:
- vectors: bfloat16 [4, 128, 256, 1024], P(None, 'vec', 'lat'), may hold values from -6 to 6
- classical_spins: float32 [3, 256, 1024], P(None, 'lat'), may hold values from -1 to 1, as said below
- coefficients: float32 [5], replicated, may hold values from 0.4 to 1.6
Outputs:
- rotated_spins: float32 [3, 256, 1024], P(None, 'lat')
- local_fields: float32 [3, 256, 1024], P(None, 'lat')
Inputs may be any that keep to these rules, and one draw needn't show every extreme that they name: `classical_spins`: each site's spin has unit length.
All inputs are finite; a program needn't handle non-finite values.
Results may differ from a plain program's by a relative error of at most 0.0003.
Values sent between devices are 32-bit elements; how exact they have to be, the bound alone decides.
A program may use at most 64 MiB of HBM per device.

v0:
```python
import jax
import jax.numpy as jnp
from jax import lax
from jax.sharding import PartitionSpec as P

STEPS = 4
coupling = 2.0
hopping = 1.0
inverse_bound = 1.0 / 6.5
time_step = 1.0


def with_halo(block, sides, width):
    for axis, dim in sides:
        count = lax.axis_size(axis)
        forward = [(i, i + 1) for i in range(count - 1)]
        forward.append((count - 1, 0))
        backward = [(target, source) for source, target in forward]
        low = lax.ppermute(
            lax.slice_in_dim(block, block.shape[dim] - width, None, axis=dim), axis, forward
        )
        high = lax.ppermute(lax.slice_in_dim(block, 0, width, axis=dim), axis, backward)
        block = jnp.concatenate([low, block, high], axis=dim)
    return block


def exchange_term(states, spins_here):
    spin_x = spins_here[0][None]
    spin_y = spins_here[1][None]
    spin_z = spins_here[2][None]
    up_real, up_imag, down_real, down_imag = (states[0], states[1], states[2], states[3])
    return jnp.stack(
        [
            spin_z * up_real + spin_x * down_real + spin_y * down_imag,
            spin_z * up_imag + spin_x * down_imag - spin_y * down_real,
            spin_x * up_real - spin_y * up_imag - spin_z * down_real,
            spin_x * up_imag + spin_y * up_real - spin_z * down_imag,
        ]
    )


def spin_density(probes, weighted):
    along_x = jnp.sum(
        probes[0] * weighted[2]
        + probes[1] * weighted[3]
        + probes[2] * weighted[0]
        + probes[3] * weighted[1],
        axis=0,
    )
    along_y = jnp.sum(
        probes[0] * weighted[3]
        - probes[1] * weighted[2]
        - probes[2] * weighted[1]
        + probes[3] * weighted[0],
        axis=0,
    )
    along_z = jnp.sum(
        probes[0] * weighted[0]
        + probes[1] * weighted[1]
        - probes[2] * weighted[2]
        - probes[3] * weighted[3],
        axis=0,
    )
    return jnp.stack([along_x, along_y, along_z])


def rotate_spins(spins_now, fields):
    magnitude = jnp.sqrt(jnp.sum(fields * fields, axis=0))
    rotation_angle = time_step * magnitude
    cosine = jnp.cos(rotation_angle)
    sine_ratio = jnp.sinc(rotation_angle / jnp.pi)
    half_ratio = 0.5 * jnp.sinc(rotation_angle / (2.0 * jnp.pi)) ** 2
    torque = jnp.cross(fields, spins_now, axis=0)
    projection = jnp.sum(fields * spins_now, axis=0)
    return (
        cosine * spins_now
        + time_step * sine_ratio * torque
        + time_step * time_step * half_ratio * projection * fields
    )


def apply_hamiltonian(padded, spins_here):
    middle = padded[:, :, 1:-1]
    neighbours = (
        padded[:, :, 2:] + padded[:, :, :-2] + jnp.roll(middle, 1, 3) + jnp.roll(middle, -1, 3)
    )
    return inverse_bound * (coupling * exchange_term(middle, spins_here) - hopping * neighbours)


def shards(vectors, classical_spins, coefficients):
    probes = vectors.astype(jnp.float32)
    count_all = vectors.shape[1] * lax.axis_size("vec")
    moments = coefficients[0] * probes
    previous = probes
    current = probes
    for degree in range(STEPS):
        padded = with_halo(current, (("lat", 2),), 1)
        following = apply_hamiltonian(padded, classical_spins)
        if degree > 0:
            following = 2.0 * following - previous
        moments = moments + coefficients[degree + 1] * following
        previous = current
        current = following
    partial_value = spin_density(probes, moments) * (coupling / count_all)
    fields = lax.psum(partial_value, "vec")
    rotated = rotate_spins(classical_spins, fields)
    return (rotated, fields)


def solution(mesh):
    placed = (P(None, "vec", "lat", None), P(None, "lat", None), P())
    return jax.shard_map(
        shards,
        mesh=mesh,
        in_specs=placed,
        out_specs=(P(None, "lat", None), P(None, "lat", None)),
        check_vma=False,
    )
```

profile of v0, /device:TPU:0, one launch (start us, length us, event | category | flops | bytes accessed | tf_op | source)
XLA Modules:
  0.0 194.6 jit_solution(3503848978186060714)
XLA Ops:
  7.2 0.0 all-reduce.2.cloned.1.call-start
  7.2 2.8 %copy_convert_fusion = f32[4,16,16,1024]{3,1,2,0:T(8,128)S(1)} fusion(bf16[4,16,16,1024]{3,2,1,0:T(8,128)(2,1)} %param.4), kind=kLoop, calls=%fused_computation.36 | loop fusion | flops 1048576 | bytes 6291456 | tf_op jit(solution)/shard_map/convert_element_type | solution.py:91
  10.1 0.1 collective-permute-start.1
  10.2 0.0 copy-start.2
  10.2 0.0 copy-start.3
  10.2 4.6 %collective-permute-start = (f32[4,16,1,1024]{3,1,2,0:T(8,128)S(1)}, f32[4,16,1,1024]{3,1,2,0:T(8,128)S(1)}, u32[]{:S(2)}, u32[]{:S(2)}) collective-permute-start(f32[4,16,1,1024]{3,1,2,0:T(8,128)S(1)} %get-tuple-element.44), channel_id=1, source_target_pairs={{8,0},{16,8},{24,16},{32,24},{40,32},{48,40},{56,48},{64,56},{72,6... | collective-permute-start | bytes 786440 | tf_op jit(solution)/shard_map/ppermute | solution.py:22
  14.8 1.7 fusion.65
  16.5 0.0 copy-done.2
  16.5 0.6 fusion.66
  17.7 0.9 multiply_add_fusion.3
  18.6 0.2 fusion.64
  18.8 0.1 collective-permute-done.1
  18.9 0.0 collective-permute-done
  19.0 4.2 %broadcast_multiply_fusion = (f32[4,16,16,1024]{3,1,2,0:T(8,128)S(1)}, f32[4,16,16,1024]{3,1,2,0:T(8,128)}) fusion(f32[4,16,16,1]{3,1,2,0:T(8,128)S(1)} %get-tuple-element.47, f32[4,16,16,1023]{3,1,2,0:T(8,128)S(1)} %get-tuple-element.49, f32[4,16,16,1023]{3,1,2,0:T(8,128)S(1)} %get-tuple-element.48, f32[4,16,16,1]{3,1,2,0:T(8,128)S(1)} %get-tuple-element.46, ...), kind=kLoop, calls=%fused_computation.37 | loop fusion | flops 13631488 | bytes 25690112 | tf_op jit(solution)/shard_map/mul | solution.py:87
  23.2 2.1 %multiply_add_fusion.2 = (f32[1,16,16,1024]{3,1,2,0:T(8,128)S(1)}, f32[1,16,16,1024]{3,1,2,0:T(8,128)S(1)}, f32[1,16,16,1024]{3,1,2,0:T(8,128)}, f32[1,16,16,1024]{3,1,2,0:T(8,128)}) fusion(f32[4,16,16,1024]{3,1,2,0:T(8,128)S(1)} %get-tuple-element.7, f32[16,1024]{1,0:T(8,128)S(1)} %get-tuple-element.54, f32[16,1024]{1,0:T(8,128)S(1)} %get-tuple-element.55, ...), kind=kLoop, calls=%fused_computation.52 | loop fusion | flops 5242880 | bytes 8585216 | tf_op jit(solution)/shard_map/add | solution.py:34
  25.3 3.4 %fusion.60 = (f32[4,16,16,1023]{3,1,2,0:T(8,128)S(1)}, f32[4,16,16,1023]{3,1,2,0:T(8,128)}) fusion(f32[4,16,16,1024]{3,1,2,0:T(8,128)S(1)} %get-tuple-element.7), kind=kLoop, calls=%fused_computation.125 | loop fusion | bytes 16760832 | tf_op jit(solution)/shard_map/jit(_roll_static)/slice | solution.py:85
  28.7 1.1 collective-permute-start.3
  29.8 2.7 %collective-permute-start.2 = (f32[4,16,1,1024]{3,1,2,0:T(8,128)S(1)}, f32[4,16,1,1024]{3,1,2,0:T(8,128)S(1)}, u32[]{:S(2)}, u32[]{:S(2)}) collective-permute-start(f32[4,16,1,1024]{3,1,2,0:T(8,128)S(1)} %get-tuple-element.42), channel_id=1, source_target_pairs={{8,0},{16,8},{24,16},{32,24},{40,32},{48,40},{56,48},{64,56},{72,6... | collective-permute-start | bytes 786440 | tf_op jit(solution)/shard_map/ppermute | solution.py:22
  32.6 0.2 fusion.61
  32.8 5.3 %collective-permute-done.3 = f32[4,16,1,1024]{3,1,2,0:T(8,128)S(1)} collective-permute-done((f32[4,16,1,1024]{3,1,2,0:T(8,128)S(1)}, f32[4,16,1,1024]{3,1,2,0:T(8,128)S(1)}, u32[]{:S(2)}, u32[]{:S(2)}) %collective-permute-start.3) | collective-permute-done | bytes 262176 | tf_op jit(solution)/shard_map/ppermute | solution.py:19
  38.1 0.0 collective-permute-done.2
  38.1 0.0 copy-done.1
  38.1 5.5 %fusion.19 = f32[4,16,16,1024]{3,1,2,0:T(8,128)S(1)} fusion(f32[4,16,16,1024]{3,1,2,0:T(8,128)S(1)} %get-tuple-element.7, f32[4,16,1,1024]{3,1,2,0:T(8,128)S(1)} %collective-permute-done.3, f32[4,16,1,1024]{3,1,2,0:T(8,128)S(1)} %collective-permute-done.2, f32[1,16,16,1024]{3,1,2,0:T(8,128)} %get-tuple-element.21, f32[1,16,16,1024]{3,1,2,0:T(8,128)} %get-tuple-element.20, ...), kind=kLoop, calls=%fused_computation.24 | loop fusion | flops 15728640 | bytes 23592960 | tf_op jit(solution)/shard_map/sub | solution.py:100
  43.6 0.7 multiply_add_fusion.1
  44.4 4.7 %fusion.57 = (f32[4,16,16,1023]{3,1,2,0:T(8,128)}, f32[4,16,16,1023]{3,1,2,0:T(8,128)}) fusion(f32[4,16,16,1024]{3,1,2,0:T(8,128)S(1)} %fusion.19), kind=kLoop, calls=%fused_computation.122 | loop fusion | bytes 16760832 | tf_op jit(solution)/shard_map/jit(_roll_static)/slice | solution.py:85
  49.0 0.1 collective-permute-start.5
  49.1 3.7 %collective-permute-start.4 = (f32[4,16,1,1024]{3,1,2,0:T(8,128)S(1)}, f32[4,16,1,1024]{3,1,2,0:T(8,128)S(1)}, u32[]{:S(2)}, u32[]{:S(2)}) collective-permute-start(f32[4,16,1,1024]{3,1,2,0:T(8,128)S(1)} %get-tuple-element.36), channel_id=1, source_target_pairs={{8,0},{16,8},{24,16},{32,24},{40,32},{48,40},{56,48},{64,56},{72,6... | collective-permute-start | bytes 786440 | tf_op jit(solution)/shard_map/ppermute | solution.py:22
  52.9 0.2 fusion.58
  53.1 6.2 %collective-permute-done.5 = f32[4,16,1,1024]{3,1,2,0:T(8,128)S(1)} collective-permute-done((f32[4,16,1,1024]{3,1,2,0:T(8,128)S(1)}, f32[4,16,1,1024]{3,1,2,0:T(8,128)S(1)}, u32[]{:S(2)}, u32[]{:S(2)}) %collective-permute-start.5) | collective-permute-done | bytes 262176 | tf_op jit(solution)/shard_map/ppermute | solution.py:19
  59.3 0.0 collective-permute-done.4
  59.3 5.4 %fusion.13 = f32[4,16,16,1024]{3,1,2,0:T(8,128)S(1)} fusion(f32[4,16,16,1024]{3,1,2,0:T(8,128)S(1)} %fusion.19, f32[4,16,1,1024]{3,1,2,0:T(8,128)S(1)} %collective-permute-done.5, f32[4,16,1,1024]{3,1,2,0:T(8,128)S(1)} %collective-permute-done.4, f32[1,16,16,1024]{3,1,2,0:T(8,128)S(1)} %get-tuple-element.17, f32[1,16,16,1024]{3,1,2,0:T(8,128)S(1)} %get-tuple-element.16, ...), kind=kLoop, calls=%fused_computation.16 | loop fusion | flops 15728640 | bytes 25690112 | tf_op jit(solution)/shard_map/sub | solution.py:100
  64.7 2.4 %multiply_add_fusion = (f32[1,16,16,1024]{3,1,2,0:T(8,128)S(1)}, f32[1,16,16,1024]{3,1,2,0:T(8,128)}, f32[1,16,16,1024]{3,1,2,0:T(8,128)}, f32[1,16,16,1024]{3,1,2,0:T(8,128)}) fusion(f32[4,16,16,1024]{3,1,2,0:T(8,128)S(1)} %fusion.13, f32[16,1024]{1,0:T(8,128)S(1)} %get-tuple-element.54, f32[16,1024]{1,0:T(8,128)S(1)} %get-tuple-element.55, ...), kind=kLoop, calls=%fused_computation.44 | loop fusion | flops 5242880 | bytes 8585216 | tf_op jit(solution)/shard_map/add | solution.py:34
  67.1 4.7 %fusion.54 = (f32[4,16,16,1023]{3,1,2,0:T(8,128)}, f32[4,16,16,1023]{3,1,2,0:T(8,128)}) fusion(f32[4,16,16,1024]{3,1,2,0:T(8,128)S(1)} %fusion.13), kind=kLoop, calls=%fused_computation.119 | loop fusion | bytes 16760832 | tf_op jit(solution)/shard_map/jit(_roll_static)/slice | solution.py:85
  71.8 0.0 collective-permute-start.7
  71.8 3.9 %collective-permute-start.6 = (f32[4,16,1,1024]{3,1,2,0:T(8,128)S(1)}, f32[4,16,1,1024]{3,1,2,0:T(8,128)}, u32[]{:S(2)}, u32[]{:S(2)}) collective-permute-start(f32[4,16,1,1024]{3,1,2,0:T(8,128)S(1)} %get-tuple-element.30), channel_id=1, source_target_pairs={{8,0},{16,8},{24,16},{32,24},{40,32},{48,40},{56,48},{64,56},{72,6... | collective-permute-start | bytes 786440 | tf_op jit(solution)/shard_map/ppermute | solution.py:22
  75.6 1.0 fusion.55
  76.7 4.2 %collective-permute-done.7 = f32[4,16,1,1024]{3,1,2,0:T(8,128)S(1)} collective-permute-done((f32[4,16,1,1024]{3,1,2,0:T(8,128)S(1)}, f32[4,16,1,1024]{3,1,2,0:T(8,128)S(1)}, u32[]{:S(2)}, u32[]{:S(2)}) %collective-permute-start.7) | collective-permute-done | bytes 262176 | tf_op jit(solution)/shard_map/ppermute | solution.py:19
  80.8 0.0 collective-permute-done.6
  80.8 12.2 %fusion.7 = f32[4,16,16,1024]{3,1,2,0:T(8,128)} fusion(f32[4,16,16,1024]{3,1,2,0:T(8,128)S(1)} %fusion.19, f32[4,16,16,1024]{3,1,2,0:T(8,128)S(1)} %fusion.13, f32[4,16,1,1024]{3,1,2,0:T(8,128)S(1)} %collective-permute-done.7, f32[4,16,1,1024]{3,1,2,0:T(8,128)} %collective-permute-done.6, f32[1,16,16,1024]{3,1,2,0:T(8,128)} %get-tuple-element.13, ...), kind=kLoop, calls=%fused_computation.8 | loop fusion | flops 25165824 | bytes 31981588 | tf_op jit(solution)/shard_map/add | solution.py:101
  93.1 3.5 %add_reduce_fusion.1 = (f32[16,1024]{1,0:T(8,128)S(1)}, f32[16,1024]{1,0:T(8,128)S(1)}, f32[16,1024]{1,0:T(8,128)S(1)}) fusion(f32[4,16,16,1024]{3,1,2,0:T(8,128)} %fusion.7, f32[4,16,16,1024]{3,1,2,0:T(8,128)S(1)} %copy_convert_fusion), kind=kLoop, calls=%fused_computation.40 | loop fusion | flops 6242304 | bytes 8585216 | tf_op jit(solution)/shard_map/reduce_sum | solution.py:43
  96.6 0.7 maximum_multiply_fusion.4
  97.3 0.0 all-reduce.2.cloned.1.call-update
  97.3 84.9 %all-reduce.2.cloned.1.call-done = f32[3,16,1024]{2,1,0:T(8,128)} async-done(((f32[3,16,1024]{2,1,0:T(8,128)}), f32[3,16,1024]{2,1,0:T(8,128)}) %all-reduce.2.cloned.1.call-update) | async-done | bytes 196624 | tf_op jit(solution)/shard_map/psum | solution.py:105
  182.2 0.9 subtract_bitcast_fusion.2
  183.1 1.0 multiply_reduce_fusion.1
  184.1 0.4 sqrt_cosine_fusion
  184.5 1.7 fusion.25
  186.2 1.6 copy.12
  (9 shorter events, 0.2 us)
Async XLA Ops:
  7.2 175.0 %all-reduce.2.cloned.1.call-start = ((), (), s32[]{:S(2)}) async-start(), calls=%async_computation | async-start | bytes 393216 | tf_op jit(solution)/shard_map/psum | solution.py:105
  10.1 8.9 %collective-permute-start.1 = (f32[4,16,1,1024]{3,1,2,0:T(8,128)S(1)}, f32[4,16,1,1024]{3,1,2,0:T(8,128)S(1)}, u32[]{:S(2)}, u32[]{:S(2)}) collective-permute-start(f32[4,16,1,1024]{3,1,2,0:T(8,128)S(1)} %get-tuple-element.45), channel_id=1, source_target_pairs={{0,8},{8,16},{16,24},{24,32},{32,40},{40,48},{48,56},{56,64},{64,7... | collective-permute-start | bytes 786440 | tf_op jit(solution)/shard_map/ppermute | solution.py:19
  10.2 6.3 %copy-start.2 = (f32[3,16,1024]{2,1,0:T(8,128)S(1)}, f32[3,16,1024]{2,1,0:T(8,128)}, u32[]{:S(2)}) copy-start(f32[3,16,1024]{2,1,0:T(8,128)} %param.5) | copy-start | bytes 589828
  10.2 6.3 %copy-start.3 = (f32[5]{0:T(128)S(1)}, f32[5]{0:T(128)}, u32[]{:S(2)}) copy-start(f32[5]{0:T(128)} %param.6) | copy-start | bytes 64
  10.2 8.7 %collective-permute-start = (f32[4,16,1,1024]{3,1,2,0:T(8,128)S(1)}, f32[4,16,1,1024]{3,1,2,0:T(8,128)S(1)}, u32[]{:S(2)}, u32[]{:S(2)}) collective-permute-start(f32[4,16,1,1024]{3,1,2,0:T(8,128)S(1)} %get-tuple-element.44), channel_id=1, source_target_pairs={{8,0},{16,8},{24,16},{32,24},{40,32},{48,40},{56,48},{64,56},{72,6... | collective-permute-start | bytes 786440 | tf_op jit(solution)/shard_map/ppermute | solution.py:22
  25.3 12.8 %copy-start.1 = (bf16[4,16,16,1024]{3,2,1,0:T(8,128)(2,1)S(1)}, bf16[4,16,16,1024]{3,2,1,0:T(8,128)(2,1)}, u32[]{:S(2)}) copy-start(bf16[4,16,16,1024]{3,2,1,0:T(8,128)(2,1)} %param.4) | copy-start | bytes 6291460
  28.7 9.4 %collective-permute-start.3 = (f32[4,16,1,1024]{3,1,2,0:T(8,128)S(1)}, f32[4,16,1,1024]{3,1,2,0:T(8,128)S(1)}, u32[]{:S(2)}, u32[]{:S(2)}) collective-permute-start(f32[4,16,1,1024]{3,1,2,0:T(8,128)S(1)} %get-tuple-element.43), channel_id=1, source_target_pairs={{0,8},{8,16},{16,24},{24,32},{32,40},{40,48},{48,56},{56,64},{64,7... | collective-permute-start | bytes 786440 | tf_op jit(solution)/shard_map/ppermute | solution.py:19
  29.8 8.3 %collective-permute-start.2 = (f32[4,16,1,1024]{3,1,2,0:T(8,128)S(1)}, f32[4,16,1,1024]{3,1,2,0:T(8,128)S(1)}, u32[]{:S(2)}, u32[]{:S(2)}) collective-permute-start(f32[4,16,1,1024]{3,1,2,0:T(8,128)S(1)} %get-tuple-element.42), channel_id=1, source_target_pairs={{8,0},{16,8},{24,16},{32,24},{40,32},{48,40},{56,48},{64,56},{72,6... | collective-permute-start | bytes 786440 | tf_op jit(solution)/shard_map/ppermute | solution.py:22
  44.4 14.9 %copy-start = (f32[4,16,16,1024]{3,1,2,0:T(8,128)S(1)}, f32[4,16,16,1024]{3,1,2,0:T(8,128)}, u32[]{:S(2)}) copy-start(f32[4,16,16,1024]{3,1,2,0:T(8,128)} %get-tuple-element.8) | copy-start | bytes 12582916
  49.0 10.3 %collective-permute-start.5 = (f32[4,16,1,1024]{3,1,2,0:T(8,128)S(1)}, f32[4,16,1,1024]{3,1,2,0:T(8,128)S(1)}, u32[]{:S(2)}, u32[]{:S(2)}) collective-permute-start(f32[4,16,1,1024]{3,1,2,0:T(8,128)S(1)} %get-tuple-element.37), channel_id=1, source_target_pairs={{0,8},{8,16},{16,24},{24,32},{32,40},{40,48},{48,56},{56,64},{64,7... | collective-permute-start | bytes 786440 | tf_op jit(solution)/shard_map/ppermute | solution.py:19
  49.1 10.1 %collective-permute-start.4 = (f32[4,16,1,1024]{3,1,2,0:T(8,128)S(1)}, f32[4,16,1,1024]{3,1,2,0:T(8,128)S(1)}, u32[]{:S(2)}, u32[]{:S(2)}) collective-permute-start(f32[4,16,1,1024]{3,1,2,0:T(8,128)S(1)} %get-tuple-element.36), channel_id=1, source_target_pairs={{8,0},{16,8},{24,16},{32,24},{40,32},{48,40},{56,48},{64,56},{72,6... | collective-permute-start | bytes 786440 | tf_op jit(solution)/shard_map/ppermute | solution.py:22
  71.8 9.1 %collective-permute-start.7 = (f32[4,16,1,1024]{3,1,2,0:T(8,128)S(1)}, f32[4,16,1,1024]{3,1,2,0:T(8,128)S(1)}, u32[]{:S(2)}, u32[]{:S(2)}) collective-permute-start(f32[4,16,1,1024]{3,1,2,0:T(8,128)S(1)} %get-tuple-element.31), channel_id=1, source_target_pairs={{0,8},{8,16},{16,24},{24,32},{32,40},{40,48},{48,56},{56,64},{64,7... | collective-permute-start | bytes 786440 | tf_op jit(solution)/shard_map/ppermute | solution.py:19
  71.8 9.1 %collective-permute-start.6 = (f32[4,16,1,1024]{3,1,2,0:T(8,128)S(1)}, f32[4,16,1,1024]{3,1,2,0:T(8,128)}, u32[]{:S(2)}, u32[]{:S(2)}) collective-permute-start(f32[4,16,1,1024]{3,1,2,0:T(8,128)S(1)} %get-tuple-element.30), channel_id=1, source_target_pairs={{8,0},{16,8},{24,16},{32,24},{40,32},{48,40},{56,48},{64,56},{72,6... | collective-permute-start | bytes 786440 | tf_op jit(solution)/shard_map/ppermute | solution.py:22
Sparse Core Ops, SparseCore 0:
  97.4 84.7 all-reduce.1
where the time goes:
time: 195 us
  waiting for transfers between devices  101 us (52%)
  other arithmetic  44.4 us (23%)
  local copies, waits for them, and re-layouts  18.4 us (9%)
  starting transfers between devices  16.3 us (8%)
  between operations  14.8 us (8%)
    psum x1, waiting for transfers between devices, shards(): fields = lax.psum(partial_value, 'vec')  84.9 us
    ppermute x4, waiting for transfers between devices, with_halo(): lax.ppermute(lax.slice_in_dim(block, block.shape[dim] - width, None, axis...  15.8 us
    ppermute x4, starting transfers between devices, with_halo(): lax.ppermute(lax.slice_in_dim(block, 0, width, axis=dim), axis, backward)  14.9 us
    slice x6, local copies, waits for them, and re-layouts, apply_hamiltonian(): jnp.roll(middle, -1, 3)  14.1 us
    add x1, other arithmetic, shards(): moments = moments + coefficients[degree + 1] * following  12.2 us
    sub x2, other arithmetic, shards(): following = 2.0 * following - previous  10.8 us
    add x4, other arithmetic, exchange_term(): spin_z * up_real + spin_x * down_real + spin_y * down_imag  6.17 us
    mul x1, other arithmetic, apply_hamiltonian(): inverse_bound * (coupling * exchange_term(middle, spins_here) - hopping *...  4.23 us
  transfers between devices with their start and end apart: 9, of which 5 were waited for; matrix products, arithmetic and copies ran while one was open for 2% of the time, Pallas kernels for 0%

commit v1 on v0

--- a/solution.py
+++ b/solution.py
@@ -102,7 +102,7 @@
         previous = current
         current = following
     partial_value = spin_density(probes, moments) * (coupling / count_all)
-    fields = lax.psum(partial_value, "vec")
+    fields = jnp.sum(lax.all_gather(partial_value, "vec"), axis=0)
     rotated = rotate_spins(classical_spins, fields)
     return (rotated, fields)
 

time: 195 us -> 156 us (0.80)
  waiting for transfers between devices: 101 us -> 65.2 us
    psum x1 -> x0, waiting for transfers between devices: 84.9 us -> none  [shards(): fields = lax.psum(partial_value, 'vec')]
    all_gather x0 -> x1, waiting for transfers between devices: none -> 49.4 us  [shards(): fields = jnp.sum(lax.all_gather(partial_value, 'vec'), axis=0)]
  transfers between devices with their start and end apart: 9 -> 9, of which waited for: 5 -> 5; matrix products, arithmetic and copies ran while one was open for 2% -> 3% of each run, Pallas kernels for 0% -> 0%
where the time goes in v1:
time: 156 us
  waiting for transfers between devices  65.2 us (42%)
  other arithmetic  43.1 us (28%)
  local copies, waits for them, and re-layouts  16.8 us (11%)
  starting transfers between devices  16.3 us (10%)
  between operations  14.8 us (9%)
    all_gather x1, waiting for transfers between devices, shards(): fields = jnp.sum(lax.all_gather(partial_value, 'vec'), axis=0)  49.4 us
    ppermute x4, waiting for transfers between devices, with_halo(): lax.ppermute(lax.slice_in_dim(block, block.shape[dim] - width, None, axis...  15.8 us
    ppermute x4, starting transfers between devices, with_halo(): lax.ppermute(lax.slice_in_dim(block, 0, width, axis=dim), axis, backward)  14.9 us
    slice x6, local copies, waits for them, and re-layouts, apply_hamiltonian(): jnp.roll(middle, -1, 3)  14.1 us
    add x1, other arithmetic, shards(): moments = moments + coefficients[degree + 1] * following  12.2 us
    sub x2, other arithmetic, shards(): following = 2.0 * following - previous  10.8 us
    add x4, other arithmetic, exchange_term(): spin_z * up_real + spin_x * down_real + spin_y * down_imag  6.19 us
    mul x1, other arithmetic, apply_hamiltonian(): inverse_bound * (coupling * exchange_term(middle, spins_here) - hopping *...  4.18 us
  transfers between devices with their start and end apart: 9, of which 5 were waited for; matrix products, arithmetic and copies ran while one was open for 3% of the time, Pallas kernels for 0%

profile of v1, /device:TPU:0, one launch (start us, length us, event | category | flops | bytes accessed | tf_op | source)
XLA Modules:
  0.0 156.2 jit_solution(1615330516895598872)
XLA Ops:
  7.2 0.0 all-gather.2.cloned.1.call-start
  7.2 2.8 %copy_convert_fusion = f32[4,16,16,1024]{3,1,2,0:T(8,128)S(1)} fusion(bf16[4,16,16,1024]{3,2,1,0:T(8,128)(2,1)} %param.4), kind=kLoop, calls=%fused_computation.36 | loop fusion | flops 1048576 | bytes 6291456 | tf_op jit(solution)/shard_map/convert_element_type | solution.py:91
  10.1 0.1 collective-permute-start.1
  10.2 0.0 copy-start.2
  10.2 0.0 copy-start.4
  10.2 4.6 %collective-permute-start = (f32[4,16,1,1024]{3,1,2,0:T(8,128)S(1)}, f32[4,16,1,1024]{3,1,2,0:T(8,128)S(1)}, u32[]{:S(2)}, u32[]{:S(2)}) collective-permute-start(f32[4,16,1,1024]{3,1,2,0:T(8,128)S(1)} %get-tuple-element.44), channel_id=1, source_target_pairs={{8,0},{16,8},{24,16},{32,24},{40,32},{48,40},{56,48},{64,56},{72,6... | collective-permute-start | bytes 786440 | tf_op jit(solution)/shard_map/ppermute | solution.py:22
  14.8 1.7 %fusion.65 = (f32[4,16,16,1023]{3,1,2,0:T(8,128)S(1)}, f32[4,16,16,1023]{3,1,2,0:T(8,128)S(1)}) fusion(f32[4,16,16,1024]{3,1,2,0:T(8,128)S(1)} %copy_convert_fusion), kind=kLoop, calls=%fused_computation.130 | loop fusion | bytes 16760832 | tf_op jit(solution)/shard_map/jit(_roll_static)/slice | solution.py:85
  16.5 0.0 copy-done.2
  16.5 0.0 copy-done.4
  16.5 0.6 fusion.66
  17.8 0.9 multiply_add_fusion.3
  18.7 0.2 fusion.64
  18.9 0.1 collective-permute-done.1
  18.9 0.0 collective-permute-done
  19.0 4.2 %broadcast_multiply_fusion = (f32[4,16,16,1024]{3,1,2,0:T(8,128)S(1)}, f32[4,16,16,1024]{3,1,2,0:T(8,128)}) fusion(f32[4,16,16,1]{3,1,2,0:T(8,128)S(1)} %get-tuple-element.47, f32[4,16,16,1023]{3,1,2,0:T(8,128)S(1)} %get-tuple-element.49, f32[4,16,16,1023]{3,1,2,0:T(8,128)S(1)} %get-tuple-element.48, f32[4,16,16,1]{3,1,2,0:T(8,128)S(1)} %get-tuple-element.46, ...), kind=kLoop, calls=%fused_computation.37 | loop fusion | flops 13631488 | bytes 25690112 | tf_op jit(solution)/shard_map/mul | solution.py:87
  23.2 2.1 %multiply_add_fusion.2 = (f32[1,16,16,1024]{3,1,2,0:T(8,128)S(1)}, f32[1,16,16,1024]{3,1,2,0:T(8,128)S(1)}, f32[1,16,16,1024]{3,1,2,0:T(8,128)}, f32[1,16,16,1024]{3,1,2,0:T(8,128)}) fusion(f32[4,16,16,1024]{3,1,2,0:T(8,128)S(1)} %get-tuple-element.7, f32[16,1024]{1,0:T(8,128)S(1)} %get-tuple-element.54, f32[16,1024]{1,0:T(8,128)S(1)} %get-tuple-element.55, ...), kind=kLoop, calls=%fused_computation.52 | loop fusion | flops 5242880 | bytes 8585216 | tf_op jit(solution)/shard_map/add | solution.py:34
  25.3 3.4 %fusion.60 = (f32[4,16,16,1023]{3,1,2,0:T(8,128)S(1)}, f32[4,16,16,1023]{3,1,2,0:T(8,128)}) fusion(f32[4,16,16,1024]{3,1,2,0:T(8,128)S(1)} %get-tuple-element.7), kind=kLoop, calls=%fused_computation.125 | loop fusion | bytes 16760832 | tf_op jit(solution)/shard_map/jit(_roll_static)/slice | solution.py:85
  28.7 1.1 collective-permute-start.3
  29.8 2.7 %collective-permute-start.2 = (f32[4,16,1,1024]{3,1,2,0:T(8,128)S(1)}, f32[4,16,1,1024]{3,1,2,0:T(8,128)S(1)}, u32[]{:S(2)}, u32[]{:S(2)}) collective-permute-start(f32[4,16,1,1024]{3,1,2,0:T(8,128)S(1)} %get-tuple-element.42), channel_id=1, source_target_pairs={{8,0},{16,8},{24,16},{32,24},{40,32},{48,40},{56,48},{64,56},{72,6... | collective-permute-start | bytes 786440 | tf_op jit(solution)/shard_map/ppermute | solution.py:22
  32.6 0.2 fusion.61
  32.8 5.3 %collective-permute-done.3 = f32[4,16,1,1024]{3,1,2,0:T(8,128)S(1)} collective-permute-done((f32[4,16,1,1024]{3,1,2,0:T(8,128)S(1)}, f32[4,16,1,1024]{3,1,2,0:T(8,128)S(1)}, u32[]{:S(2)}, u32[]{:S(2)}) %collective-permute-start.3) | collective-permute-done | bytes 262176 | tf_op jit(solution)/shard_map/ppermute | solution.py:19
  38.1 0.0 collective-permute-done.2
  38.1 5.5 %fusion.19 = f32[4,16,16,1024]{3,1,2,0:T(8,128)S(1)} fusion(f32[4,16,16,1024]{3,1,2,0:T(8,128)S(1)} %get-tuple-element.7, f32[4,16,1,1024]{3,1,2,0:T(8,128)S(1)} %collective-permute-done.3, f32[4,16,1,1024]{3,1,2,0:T(8,128)S(1)} %collective-permute-done.2, f32[1,16,16,1024]{3,1,2,0:T(8,128)} %get-tuple-element.21, f32[1,16,16,1024]{3,1,2,0:T(8,128)} %get-tuple-element.20, ...), kind=kLoop, calls=%fused_computation.24 | loop fusion | flops 15728640 | bytes 23592960 | tf_op jit(solution)/shard_map/sub | solution.py:100
  43.6 0.7 multiply_add_fusion.1
  44.3 0.0 copy-start
  44.3 4.7 %fusion.57 = (f32[4,16,16,1023]{3,1,2,0:T(8,128)}, f32[4,16,16,1023]{3,1,2,0:T(8,128)}) fusion(f32[4,16,16,1024]{3,1,2,0:T(8,128)S(1)} %fusion.19), kind=kLoop, calls=%fused_computation.122 | loop fusion | bytes 16760832 | tf_op jit(solution)/shard_map/jit(_roll_static)/slice | solution.py:85
  49.0 0.1 collective-permute-start.5
  49.1 3.7 %collective-permute-start.4 = (f32[4,16,1,1024]{3,1,2,0:T(8,128)S(1)}, f32[4,16,1,1024]{3,1,2,0:T(8,128)S(1)}, u32[]{:S(2)}, u32[]{:S(2)}) collective-permute-start(f32[4,16,1,1024]{3,1,2,0:T(8,128)S(1)} %get-tuple-element.36), channel_id=1, source_target_pairs={{8,0},{16,8},{24,16},{32,24},{40,32},{48,40},{56,48},{64,56},{72,6... | collective-permute-start | bytes 786440 | tf_op jit(solution)/shard_map/ppermute | solution.py:22
  52.8 0.2 fusion.58
  53.0 6.2 %collective-permute-done.5 = f32[4,16,1,1024]{3,1,2,0:T(8,128)S(1)} collective-permute-done((f32[4,16,1,1024]{3,1,2,0:T(8,128)S(1)}, f32[4,16,1,1024]{3,1,2,0:T(8,128)S(1)}, u32[]{:S(2)}, u32[]{:S(2)}) %collective-permute-start.5) | collective-permute-done | bytes 262176 | tf_op jit(solution)/shard_map/ppermute | solution.py:19
  59.2 0.0 collective-permute-done.4
  59.2 5.4 %fusion.13 = f32[4,16,16,1024]{3,1,2,0:T(8,128)S(1)} fusion(f32[4,16,16,1024]{3,1,2,0:T(8,128)S(1)} %fusion.19, f32[4,16,1,1024]{3,1,2,0:T(8,128)S(1)} %collective-permute-done.5, f32[4,16,1,1024]{3,1,2,0:T(8,128)S(1)} %collective-permute-done.4, f32[1,16,16,1024]{3,1,2,0:T(8,128)S(1)} %get-tuple-element.17, f32[1,16,16,1024]{3,1,2,0:T(8,128)S(1)} %get-tuple-element.16, ...), kind=kLoop, calls=%fused_computation.16 | loop fusion | flops 15728640 | bytes 25690112 | tf_op jit(solution)/shard_map/sub | solution.py:100
  64.7 2.4 %multiply_add_fusion = (f32[1,16,16,1024]{3,1,2,0:T(8,128)S(1)}, f32[1,16,16,1024]{3,1,2,0:T(8,128)}, f32[1,16,16,1024]{3,1,2,0:T(8,128)}, f32[1,16,16,1024]{3,1,2,0:T(8,128)}) fusion(f32[4,16,16,1024]{3,1,2,0:T(8,128)S(1)} %fusion.13, f32[16,1024]{1,0:T(8,128)S(1)} %get-tuple-element.54, f32[16,1024]{1,0:T(8,128)S(1)} %get-tuple-element.55, ...), kind=kLoop, calls=%fused_computation.44 | loop fusion | flops 5242880 | bytes 8585216 | tf_op jit(solution)/shard_map/add | solution.py:34
  67.1 4.6 %fusion.54 = (f32[4,16,16,1023]{3,1,2,0:T(8,128)}, f32[4,16,16,1023]{3,1,2,0:T(8,128)}) fusion(f32[4,16,16,1024]{3,1,2,0:T(8,128)S(1)} %fusion.13), kind=kLoop, calls=%fused_computation.119 | loop fusion | bytes 16760832 | tf_op jit(solution)/shard_map/jit(_roll_static)/slice | solution.py:85
  71.8 0.0 collective-permute-start.7
  71.8 3.9 %collective-permute-start.6 = (f32[4,16,1,1024]{3,1,2,0:T(8,128)S(1)}, f32[4,16,1,1024]{3,1,2,0:T(8,128)}, u32[]{:S(2)}, u32[]{:S(2)}) collective-permute-start(f32[4,16,1,1024]{3,1,2,0:T(8,128)S(1)} %get-tuple-element.30), channel_id=1, source_target_pairs={{8,0},{16,8},{24,16},{32,24},{40,32},{48,40},{56,48},{64,56},{72,6... | collective-permute-start | bytes 786440 | tf_op jit(solution)/shard_map/ppermute | solution.py:22
  75.6 1.0 fusion.55
  76.6 4.2 %collective-permute-done.7 = f32[4,16,1,1024]{3,1,2,0:T(8,128)S(1)} collective-permute-done((f32[4,16,1,1024]{3,1,2,0:T(8,128)S(1)}, f32[4,16,1,1024]{3,1,2,0:T(8,128)S(1)}, u32[]{:S(2)}, u32[]{:S(2)}) %collective-permute-start.7) | collective-permute-done | bytes 262176 | tf_op jit(solution)/shard_map/ppermute | solution.py:19
  80.8 0.0 collective-permute-done.6
  80.8 12.2 %fusion.7 = f32[4,16,16,1024]{3,1,2,0:T(8,128)} fusion(f32[4,16,16,1024]{3,1,2,0:T(8,128)S(1)} %fusion.19, f32[4,16,16,1024]{3,1,2,0:T(8,128)S(1)} %fusion.13, f32[4,16,1,1024]{3,1,2,0:T(8,128)S(1)} %collective-permute-done.7, f32[4,16,1,1024]{3,1,2,0:T(8,128)} %collective-permute-done.6, f32[1,16,16,1024]{3,1,2,0:T(8,128)} %get-tuple-element.13, ...), kind=kLoop, calls=%fused_computation.8 | loop fusion | flops 25165824 | bytes 31981588 | tf_op jit(solution)/shard_map/add | solution.py:101
  93.0 3.5 %add_reduce_fusion.1 = (f32[16,1024]{1,0:T(8,128)S(1)}, f32[16,1024]{1,0:T(8,128)S(1)}, f32[16,1024]{1,0:T(8,128)S(1)}) fusion(f32[4,16,16,1024]{3,1,2,0:T(8,128)} %fusion.7, f32[4,16,16,1024]{3,1,2,0:T(8,128)S(1)} %copy_convert_fusion), kind=kLoop, calls=%fused_computation.40 | loop fusion | flops 6242304 | bytes 8585216 | tf_op jit(solution)/shard_map/reduce_sum | solution.py:43
  96.5 0.7 maximum_multiply_fusion.4
  97.2 0.0 all-gather.2.cloned.1.call-update
  97.2 49.4 %all-gather.2.cloned.1.call-done = f32[8,3,16,1024]{3,2,1,0:T(8,128)} async-done(((f32[1,3,16,1024]{3,2,1,0:T(8,128)}), f32[8,3,16,1024]{3,2,1,0:T(8,128)}) %all-gather.2.cloned.1.call-update) | async-done | bytes 1572880 | tf_op jit(solution)/shard_map/all_gather | solution.py:105
  146.6 1.5 reduce_sum.57
  148.1 0.0 copy-start.3
  148.2 0.4 sqrt_cosine_fusion
  148.6 0.7 fusion.25
  (11 shorter events, 0.2 us)
Async XLA Ops:
  7.2 139.4 %all-gather.2.cloned.1.call-start = ((), (), s32[]{:S(2)}) async-start(), calls=%async_computation | async-start | bytes 1769472 | tf_op jit(solution)/shard_map/all_gather | solution.py:105
  10.1 8.9 %collective-permute-start.1 = (f32[4,16,1,1024]{3,1,2,0:T(8,128)S(1)}, f32[4,16,1,1024]{3,1,2,0:T(8,128)S(1)}, u32[]{:S(2)}, u32[]{:S(2)}) collective-permute-start(f32[4,16,1,1024]{3,1,2,0:T(8,128)S(1)} %get-tuple-element.45), channel_id=1, source_target_pairs={{0,8},{8,16},{16,24},{24,32},{32,40},{40,48},{48,56},{56,64},{64,7... | collective-permute-start | bytes 786440 | tf_op jit(solution)/shard_map/ppermute | solution.py:19
  10.2 6.3 %copy-start.2 = (f32[3,16,1024]{2,1,0:T(8,128)S(1)}, f32[3,16,1024]{2,1,0:T(8,128)}, u32[]{:S(2)}) copy-start(f32[3,16,1024]{2,1,0:T(8,128)} %param.5) | copy-start | bytes 589828
  10.2 6.3 %copy-start.4 = (f32[5]{0:T(128)S(1)}, f32[5]{0:T(128)}, u32[]{:S(2)}) copy-start(f32[5]{0:T(128)} %param.6) | copy-start | bytes 64
  10.2 8.7 %collective-permute-start = (f32[4,16,1,1024]{3,1,2,0:T(8,128)S(1)}, f32[4,16,1,1024]{3,1,2,0:T(8,128)S(1)}, u32[]{:S(2)}, u32[]{:S(2)}) collective-permute-start(f32[4,16,1,1024]{3,1,2,0:T(8,128)S(1)} %get-tuple-element.44), channel_id=1, source_target_pairs={{8,0},{16,8},{24,16},{32,24},{40,32},{48,40},{56,48},{64,56},{72,6... | collective-permute-start | bytes 786440 | tf_op jit(solution)/shard_map/ppermute | solution.py:22
  25.3 12.8 %copy-start.1 = (bf16[4,16,16,1024]{3,2,1,0:T(8,128)(2,1)S(1)}, bf16[4,16,16,1024]{3,2,1,0:T(8,128)(2,1)}, u32[]{:S(2)}) copy-start(bf16[4,16,16,1024]{3,2,1,0:T(8,128)(2,1)} %param.4) | copy-start | bytes 6291460
  28.7 9.4 %collective-permute-start.3 = (f32[4,16,1,1024]{3,1,2,0:T(8,128)S(1)}, f32[4,16,1,1024]{3,1,2,0:T(8,128)S(1)}, u32[]{:S(2)}, u32[]{:S(2)}) collective-permute-start(f32[4,16,1,1024]{3,1,2,0:T(8,128)S(1)} %get-tuple-element.43), channel_id=1, source_target_pairs={{0,8},{8,16},{16,24},{24,32},{32,40},{40,48},{48,56},{56,64},{64,7... | collective-permute-start | bytes 786440 | tf_op jit(solution)/shard_map/ppermute | solution.py:19
  29.8 8.3 %collective-permute-start.2 = (f32[4,16,1,1024]{3,1,2,0:T(8,128)S(1)}, f32[4,16,1,1024]{3,1,2,0:T(8,128)S(1)}, u32[]{:S(2)}, u32[]{:S(2)}) collective-permute-start(f32[4,16,1,1024]{3,1,2,0:T(8,128)S(1)} %get-tuple-element.42), channel_id=1, source_target_pairs={{8,0},{16,8},{24,16},{32,24},{40,32},{48,40},{56,48},{64,56},{72,6... | collective-permute-start | bytes 786440 | tf_op jit(solution)/shard_map/ppermute | solution.py:22
  44.3 14.9 %copy-start = (f32[4,16,16,1024]{3,1,2,0:T(8,128)S(1)}, f32[4,16,16,1024]{3,1,2,0:T(8,128)}, u32[]{:S(2)}) copy-start(f32[4,16,16,1024]{3,1,2,0:T(8,128)} %get-tuple-element.8) | copy-start | bytes 12582916
  49.0 10.3 %collective-permute-start.5 = (f32[4,16,1,1024]{3,1,2,0:T(8,128)S(1)}, f32[4,16,1,1024]{3,1,2,0:T(8,128)S(1)}, u32[]{:S(2)}, u32[]{:S(2)}) collective-permute-start(f32[4,16,1,1024]{3,1,2,0:T(8,128)S(1)} %get-tuple-element.37), channel_id=1, source_target_pairs={{0,8},{8,16},{16,24},{24,32},{32,40},{40,48},{48,56},{56,64},{64,7... | collective-permute-start | bytes 786440 | tf_op jit(solution)/shard_map/ppermute | solution.py:19
  49.1 10.1 %collective-permute-start.4 = (f32[4,16,1,1024]{3,1,2,0:T(8,128)S(1)}, f32[4,16,1,1024]{3,1,2,0:T(8,128)S(1)}, u32[]{:S(2)}, u32[]{:S(2)}) collective-permute-start(f32[4,16,1,1024]{3,1,2,0:T(8,128)S(1)} %get-tuple-element.36), channel_id=1, source_target_pairs={{8,0},{16,8},{24,16},{32,24},{40,32},{48,40},{56,48},{64,56},{72,6... | collective-permute-start | bytes 786440 | tf_op jit(solution)/shard_map/ppermute | solution.py:22
  71.8 9.1 %collective-permute-start.7 = (f32[4,16,1,1024]{3,1,2,0:T(8,128)S(1)}, f32[4,16,1,1024]{3,1,2,0:T(8,128)S(1)}, u32[]{:S(2)}, u32[]{:S(2)}) collective-permute-start(f32[4,16,1,1024]{3,1,2,0:T(8,128)S(1)} %get-tuple-element.31), channel_id=1, source_target_pairs={{0,8},{8,16},{16,24},{24,32},{32,40},{40,48},{48,56},{56,64},{64,7... | collective-permute-start | bytes 786440 | tf_op jit(solution)/shard_map/ppermute | solution.py:19
  71.8 9.1 %collective-permute-start.6 = (f32[4,16,1,1024]{3,1,2,0:T(8,128)S(1)}, f32[4,16,1,1024]{3,1,2,0:T(8,128)}, u32[]{:S(2)}, u32[]{:S(2)}) collective-permute-start(f32[4,16,1,1024]{3,1,2,0:T(8,128)S(1)} %get-tuple-element.30), channel_id=1, source_target_pairs={{8,0},{16,8},{24,16},{32,24},{40,32},{48,40},{56,48},{64,56},{72,6... | collective-permute-start | bytes 786440 | tf_op jit(solution)/shard_map/ppermute | solution.py:22
  148.1 1.2 copy-start.3
Sparse Core Ops, SparseCore 0:
  97.3 49.2 all-gather.1
